TPU v7x, 256 devices: a whole 4x4x8 slice. The times are simulated.
256 devices in a mesh: rows: 2 (over core), sites: 8 (over z), bond: 16 (over y, x).
Axes of the slice: x: 4, y: 4, z: 8, core: 2. Of those that a mesh axis runs over, the one named last changes fastest.
Arguments:
- boundary_in: float32 [1, 8, 256, 8, 256], P(None, 'sites', None, None, 'bond'), may hold values from -6 to 6
- mpo: float32 [4, 8, 8, 8, 8, 8], P('rows', 'sites'), may hold values from -0.75 to 0.75
- proj: float32 [4, 8, 256, 8, 256], P('rows', 'sites'), may hold values from -0.125 to 0.125
Outputs:
- boundary_out: float32 [2, 1, 8, 256, 8, 256], P('rows', None, 'sites', None, None, 'bond')
All inputs are finite; a program needn't handle non-finite values.
Results may differ from a plain program's by a relative error of at most 0.00013.
Values sent between devices are 32-bit elements; how exact they have to be, the bound alone decides.
A program may use at most 64 MiB of HBM per device.

v0:
```python
import jax
import jax.numpy as jnp
from jax import lax
from jax.sharding import PartitionSpec as P


def from_behind(shard, axis, by):
    size = lax.axis_size(axis)
    return lax.ppermute(shard, axis, [(i, (i + by) % size) for i in range(size)])


def from_behind_2(shard, axis, by):
    size = lax.axis_size(axis)
    pairs = [(i, i + by) for i in range(size) if 0 <= i + by < size]
    return lax.ppermute(shard, axis, pairs)


def left_mix(left_proj, boundary, mpo_row):
    precise = lax.Precision.HIGHEST
    left_part = jnp.einsum("alx,taub->tlxub", left_proj, boundary, precision=precise)
    return jnp.einsum("tlxub,ludr->txdbr", left_part, mpo_row, precision=precise)


def body(boundary_in, mpo, proj):
    precise = lax.Precision.HIGHEST
    left_all = from_behind(proj, "sites", 1)
    half_width = boundary_in.shape[4]
    bond_pos = lax.axis_index("bond")
    rows_here = mpo.shape[0]
    group_pos = lax.axis_index("rows")
    group_count = lax.axis_size("rows")
    initial = boundary_in[:, 0]
    current = initial
    stored = jnp.zeros_like(initial)
    for section_pos in range(group_count):
        boundary = current
        for inner_row in range(rows_here):
            left_proj = left_all[inner_row, 0]
            right_proj = proj[inner_row, 0]
            mpo_row = mpo[inner_row, 0]
            mixed_rows = left_mix(left_proj, boundary, mpo_row)
            right_rows = lax.dynamic_slice_in_dim(right_proj, bond_pos * half_width, half_width, 0)
            partial_value = jnp.einsum("txdbr,bry->txdy", mixed_rows, right_rows, precision=precise)
            boundary = lax.psum_scatter(partial_value, "bond", scatter_dimension=3, tiled=True)
        entries = boundary.shape[1] * boundary.shape[2] * boundary.shape[1]
        square_sum = jnp.sum(boundary * boundary, axis=(1, 2, 3))
        norm_total = lax.psum(square_sum, "bond")
        scale = jnp.sqrt(norm_total / entries + 1e-06)
        result = boundary / scale[:, None, None, None]
        stored = jnp.where(group_pos == section_pos, result, stored)
        if section_pos + 1 < group_count:
            current = from_behind_2(result, "rows", 1)
    return stored[None, :, None]


def solution(mesh):
    return jax.shard_map(
        body,
        mesh=mesh,
        in_specs=(
            P(None, "sites", None, None, "bond"),
            P("rows", "sites", None, None, None, None),
            P("rows", "sites", None, None, None),
        ),
        out_specs=P("rows", None, "sites", None, None, "bond"),
        check_vma=False,
    )
```

profile of v0, /device:TPU:1, one launch (start us, length us, event | category | flops | bytes accessed | tf_op | source)
XLA Modules:
  0.0 543.9 jit_solution(4189467171748384423)
XLA Ops:
  6.5 0.0 copy-start
  6.5 0.0 copy-start.2
  6.5 0.0 reduce-scatter.5.cloned.1.call-start
  6.5 5.5 %copy.21 = f32[2,1,256,8,256]{4,2,3,1,0:T(8,128)} copy(f32[2,1,256,8,256]{4,3,2,1,0:T(8,128)} %param.5) | data formatting | bytes 8388608 | tf_op args[2]
  12.0 2.5 collective-permute-start
  14.5 0.0 copy-done.2
  14.5 0.1 copy.72
  14.7 2.5 fusion.24
  17.3 91.8 %collective-permute-done = f32[2,1,256,8,256]{4,2,3,1,0:T(8,128)} collective-permute-done((f32[2,1,256,8,256]{4,2,3,1,0:T(8,128)}, f32[2,1,256,8,256]{4,2,3,1,0:T(8,128)}, u32[]{:S(2)}, u32[]{:S(2)}) %collective-permute-start) | collective-permute-done | bytes 4194336 | tf_op jit(solution)/shard_map/ppermute | solution.py:9
  109.0 0.0 copy-done
  109.0 2.8 fusion.6
  111.9 1.7 convolution_bitcast_fusion.7
  113.6 3.2 convolution_bitcast_fusion.3
  116.8 3.1 copy.26
  119.9 0.0 reduce-scatter.5.cloned.1.call-update
  119.9 0.2 reduce-scatter.7.cloned.1.call-start
  120.2 0.1 copy.73
  120.4 78.0 %reduce-scatter.5.cloned.1.call-done = f32[1,256,8,16]{1,2,0,3:T(8,128)} async-done(((f32[1,256,8,256]{1,2,0,3:T(8,128)}), f32[1,256,8,16]{1,2,0,3:T(8,128)}) %reduce-scatter.5.cloned.1.call-update) | async-done | bytes 131088 | tf_op jit(solution)/shard_map/reduce_scatter | solution.py:44
  198.4 2.9 fusion.4
  201.3 1.7 convolution_bitcast_fusion.6
  203.1 1.9 convolution_bitcast_fusion.2
  204.9 2.0 copy.32
  206.9 0.0 reduce-scatter.7.cloned.1.call-update
  207.0 0.0 reduce-scatter.9.cloned.1.call-start
  207.0 78.8 %reduce-scatter.7.cloned.1.call-done = f32[1,256,8,16]{1,2,0,3:T(8,128)} async-done(((f32[1,256,8,256]{1,2,0,3:T(8,128)}), f32[1,256,8,16]{1,2,0,3:T(8,128)}) %reduce-scatter.7.cloned.1.call-update) | async-done | bytes 131088 | tf_op jit(solution)/shard_map/reduce_scatter | solution.py:44
  285.8 1.5 multiply_reduce_fusion.1
  287.4 31.5 %psum.14 = f32[1]{0:T(128)} all-reduce(f32[1]{0:T(128)} %bitcast.41), channel_id=1, replica_groups=mesh['rows'=2,'sites'=8,'bond'=16] {'bond'}, use_global_device_ids=true, to_apply=%region_3.0 | all-reduce | flops 1 | bytes 8 | tf_op jit(solution)/shard_map/psum | solution.py:47
  319.6 0.9 broadcast_divide_fusion
  320.5 1.3 collective-permute-start.1
  321.8 10.4 %collective-permute-done.1 = f32[1,256,8,16]{1,3,2,0:T(8,128)S(1)} collective-permute-done((f32[1,256,8,16]{1,3,2,0:T(8,128)S(1)}, f32[1,256,8,16]{1,3,2,0:T(8,128)S(1)}, u32[]{:S(2)}, u32[]{:S(2)}) %collective-permute-start.1) | collective-permute-done | bytes 131104 | tf_op jit(solution)/shard_map/ppermute | solution.py:15
  332.2 2.8 fusion.7
  335.0 1.7 convolution_bitcast_fusion.5
  336.8 1.9 convolution_bitcast_fusion.1
  338.6 2.0 copy.36
  340.6 0.0 reduce-scatter.9.cloned.1.call-update
  340.7 0.3 reduce-scatter.11.cloned.1.call-start
  340.9 73.6 %reduce-scatter.9.cloned.1.call-done = f32[1,256,8,16]{1,2,0,3:T(8,128)} async-done(((f32[1,256,8,256]{1,2,0,3:T(8,128)}), f32[1,256,8,16]{1,2,0,3:T(8,128)}) %reduce-scatter.9.cloned.1.call-update) | async-done | bytes 131088 | tf_op jit(solution)/shard_map/reduce_scatter | solution.py:44
  414.5 2.9 fusion.5
  417.5 1.7 convolution_bitcast_fusion.4
  419.2 1.9 convolution_bitcast_fusion
  421.1 2.0 copy.40
  423.1 0.0 reduce-scatter.11.cloned.1.call-update
  423.1 78.9 %reduce-scatter.11.cloned.1.call-done = f32[1,256,8,16]{1,2,0,3:T(8,128)} async-done(((f32[1,256,8,256]{1,2,0,3:T(8,128)}), f32[1,256,8,16]{1,2,0,3:T(8,128)}) %reduce-scatter.11.cloned.1.call-update) | async-done | bytes 131088 | tf_op jit(solution)/shard_map/reduce_scatter | solution.py:44
  502.0 1.6 multiply_reduce_fusion
  503.6 31.5 %psum.15 = f32[1]{0:T(128)} all-reduce(f32[1]{0:T(128)} %bitcast.72), channel_id=1, replica_groups=mesh['rows'=2,'sites'=8,'bond'=16] {'bond'}, use_global_device_ids=true, to_apply=%region_7.8 | all-reduce | flops 1 | bytes 8 | tf_op jit(solution)/shard_map/psum | solution.py:47
  535.7 0.0 copy-done.1
  535.7 0.9 select_bitcast_fusion
  536.7 0.7 copy.41
  (7 shorter events, 0.2 us)
Async XLA Ops:
  6.5 102.5 %copy-start = (f32[1,1,256,8,16]{2,4,3,1,0:T(8,128)S(1)}, f32[1,1,256,8,16]{2,4,3,1,0:T(8,128)}, u32[]{:S(2)}) copy-start(f32[1,1,256,8,16]{2,4,3,1,0:T(8,128)} %param.3) | copy-start | bytes 393220
  6.5 7.9 %copy-start.2 = (f32[2,1,8,8,8,8]{5,4,3,2,1,0:T(8,128)S(1)}, f32[2,1,8,8,8,8]{5,4,3,2,1,0:T(8,128)}, u32[]{:S(2)}) copy-start(f32[2,1,8,8,8,8]{5,4,3,2,1,0:T(8,128)} %param.4) | copy-start | bytes 98308
  6.5 191.8 %reduce-scatter.5.cloned.1.call-start = ((), (), s32[]{:S(2)}) async-start(), calls=%async_computation.4 | async-start | bytes 2228224 | tf_op jit(solution)/shard_map/reduce_scatter | solution.py:44
  12.0 97.0 %collective-permute-start = (f32[2,1,256,8,256]{4,2,3,1,0:T(8,128)}, f32[2,1,256,8,256]{4,2,3,1,0:T(8,128)}, u32[]{:S(2)}, u32[]{:S(2)}) collective-permute-start(f32[2,1,256,8,256]{4,2,3,1,0:T(8,128)} %copy.21), channel_id=1, source_target_pairs={{0,16},{16,32},{32,48},{48,64},{64,80},{80,96},{96,112},{112,0},{1... | collective-permute-start | bytes 12582920 | tf_op jit(solution)/shard_map/ppermute | solution.py:9
  119.9 165.9 %reduce-scatter.7.cloned.1.call-start = ((), (), s32[]{:S(2)}) async-start(), calls=%async_computation.5 | async-start | bytes 2228224 | tf_op jit(solution)/shard_map/reduce_scatter | solution.py:44
  207.0 207.6 %reduce-scatter.9.cloned.1.call-start = ((), (), s32[]{:S(2)}) async-start(), calls=%async_computation.6 | async-start | bytes 2228224 | tf_op jit(solution)/shard_map/reduce_scatter | solution.py:44
  320.5 11.7 %collective-permute-start.1 = (f32[1,256,8,16]{1,3,2,0:T(8,128)S(1)}, f32[1,256,8,16]{1,3,2,0:T(8,128)S(1)}, u32[]{:S(2)}, u32[]{:S(2)}) collective-permute-start(f32[1,256,8,16]{1,3,2,0:T(8,128)S(1)} %copy.33), channel_id=1, source_target_pairs={{0,128},{1,129},{2,130},{3,131},{4,132},{5,133},{6,134},{7,135},{8... | collective-permute-start | bytes 393224 | tf_op jit(solution)/shard_map/ppermute | solution.py:15
  340.7 161.3 %reduce-scatter.11.cloned.1.call-start = ((), (), s32[]{:S(2)}) async-start(), calls=%async_computation.7 | async-start | bytes 2228224 | tf_op jit(solution)/shard_map/reduce_scatter | solution.py:44
  423.1 112.6 %copy-start.1 = (f32[1,256,8,16]{1,2,0,3:T(8,128)S(1)}, f32[1,256,8,16]{1,2,0,3:T(8,128)}, u32[]{:S(2)}) copy-start(f32[1,256,8,16]{1,2,0,3:T(8,128)} %reduce-scatter.7.cloned.1.call-done) | copy-start | bytes 393220
Sparse Core Ops, SparseCore 0:
  120.0 78.2 reduce-scatter.4
  207.1 78.6 reduce-scatter.6
  340.8 73.6 reduce-scatter.8
  423.3 78.6 reduce-scatter.10
where the time goes:
time: 552 us; the launch traced here: 544 us
  waiting for transfers between devices  411 us (74%)
  blocking collectives  63 us (11%)
  matrix products  27.2 us (5%)
  local copies, waits for them, and re-layouts  18.3 us (3%)
  between operations  14.6 us (3%)
    reduce_scatter x4, waiting for transfers between devices, body(): lax.psum_scatter(partial_value, 'bond', scatter_dimension=3, tiled=True)  309 us
    ppermute x1, waiting for transfers between devices, from_behind(): lax.ppermute(shard, axis, [(i, (i + by) % size) for i in range(size)])  91.8 us
    psum x2, blocking collectives, body(): norm_total = lax.psum(square_sum, 'bond')  63 us
    dot_general x4, matrix products, left_mix(): jnp.einsum('alx,taub->tlxub', left_proj, boundary, precision=precise)  11.5 us
  transfers between devices with their start and end apart: 6, of which 6 were waited for; matrix products, arithmetic and copies ran while one was open for 1% of the time, Pallas kernels for 0%

commit v1 on v0

v1 whole, which is shorter than its diff:
```python
import functools

import jax
import jax.numpy as jnp
from jax import lax
from jax.experimental import pallas as pl
from jax.experimental.pallas import tpu as pltpu
from jax.sharding import PartitionSpec as P

MESH = pl.DeviceIdType.MESH
F32 = jnp.float32
BF16 = jnp.bfloat16


def halves(value):
    high = value.astype(BF16)
    return high, (value - high.astype(F32)).astype(BF16)


def dot(lhs, rhs):
    return jnp.dot(lhs, rhs, preferred_element_type=F32)


def low_lanes(rows):
    return lax.broadcasted_iota(jnp.int32, (rows, 128), 1) < 64


def pair_even(first, second):
    return jnp.where(low_lanes(first.shape[0]), first, pltpu.roll(second, 64, 1))


def pair_odd(first, second):
    return jnp.where(low_lanes(first.shape[0]), pltpu.roll(first, 64, 1), second)


def kernel(
    b_ref, p_ref, m_ref, out_ref,
    first_in, gathered, partial_in, partial, slab, squares, own_square, scale_in,
    left_stage, left_packed, left_in, right_raw, mpo_raw,
    left_high, left_low, right_parts, mpo_parts, lhs_rows, mixed_in, mixed_out,
    first_sem, gather_sem, partial_sem, slab_sem, square_sem, scale_sem,
    left_sem, right_sem, mpo_sem, stage_sem,
    first_send, gather_send, partial_send, slab_send, square_send, scale_send,
    left_send, right_send, mpo_send,
):
    core = lax.axis_index("rows")
    site = lax.axis_index("sites")
    bond = lax.axis_index("bond")
    col = lax.rem(bond, 4)
    row = bond // 4
    next_site = lax.rem(site + 1, 8)
    prev_site = lax.rem(site + 7, 8)

    def in_row(step):
        return row * 4 + lax.rem(col + step, 4)

    def in_col(step):
        return lax.rem(row + step, 4) * 4 + col

    def remote(src, dst, send, recv, device):
        return pltpu.make_async_remote_copy(
            src_ref=src, dst_ref=dst, send_sem=send, recv_sem=recv, device_id=device, device_id_type=MESH
        )

    def left_stage_copy(k):
        block = pl.ds(pl.multiple_of((col // 2) * 128, 128), 128)
        return pltpu.make_async_copy(p_ref.at[k, :, :, block], left_stage.at[k], stage_sem.at[k])

    def own_right(k):
        return p_ref.at[k, pl.ds(row * 64, 64)]

    barrier = pltpu.get_barrier_semaphore()
    peers = [(core, site, lax.rem(bond + k, 16)) for k in range(1, 16)]
    peers += [(1 - core, site, bond), (0, next_site, bond), (1, next_site, bond), (0, prev_site, bond), (1, prev_site, bond)]
    for k in range(2):
        left_stage_copy(k).start()
    for peer in peers:
        pl.semaphore_signal(barrier, inc=1, device_id=peer, device_id_type=MESH)
    pl.semaphore_wait(barrier, len(peers))

    def left_send_copy(k, pair, lattice_row):
        return remote(
            left_packed.at[k, pair], left_in.at[lattice_row, pair], left_send.at[k], left_sem.at[lattice_row, pair],
            (1, next_site, bond),
        )

    def pack_left(k, pair):
        first = left_stage[k, :, 2 * pair, :]
        second = left_stage[k, :, 2 * pair + 1, :]
        half = lax.rem(col, 2)

        @pl.when(half == 0)
        def _():
            left_packed[k, pair] = pair_even(first, second)

        @pl.when(half == 1)
        def _():
            left_packed[k, pair] = pair_odd(first, second)

    def square_copy(step):
        return remote(
            own_square, squares.at[bond], square_send, square_sem, (core, site, lax.rem(bond + step, 16))
        )

    def exchange_squares(value):
        own_square[...] = value
        squares[bond] = value
        for step in range(1, 16):
            square_copy(step).start()

    def inverse_scale():
        pltpu.make_async_copy(squares.at[pl.ds(0, 15)], squares.at[pl.ds(0, 15)], square_sem).wait()
        total = jnp.sum(squares[...])
        mean = jnp.full((8, 128), total, F32) / 524288.0
        return 1.0 / jnp.sqrt(mean + 1e-06)

    def fold(value):
        squared = value * value
        acc = jnp.zeros((8, 128), F32)
        for r0 in range(0, value.shape[0], 8):
            for c0 in range(0, 512, 128):
                acc = acc + squared[r0:r0 + 8, c0:c0 + 128]
        return acc

    def write_out(inverse):
        for r0 in (0, 8):
            for pair in range(2):
                for d_pair in range(4):
                    first = slab[2 * pair, r0:r0 + 8, d_pair * 128:d_pair * 128 + 128]
                    second = slab[2 * pair + 1, r0:r0 + 8, d_pair * 128:d_pair * 128 + 128]
                    lanes = slice(pair * 128, pair * 128 + 128)
                    out_ref[2 * d_pair, r0:r0 + 8, lanes] = pair_even(first, second) * inverse
                    out_ref[2 * d_pair + 1, r0:r0 + 8, lanes] = pair_odd(first, second) * inverse

    def wait_squares_sent():
        pltpu.make_async_copy(squares.at[pl.ds(0, 15)], squares.at[pl.ds(0, 15)], square_send).wait()

    def wait_left_sent():
        for k in range(2):
            pltpu.make_async_copy(left_packed.at[k], left_packed.at[k], left_send.at[k]).wait()

    @pl.when(core == 0)
    def _():
        partner = (1, site, bond)
        right_copies = [remote(own_right(k), right_raw.at[k], right_send.at[k], right_sem.at[k], partner) for k in range(2)]
        mpo_copies = [remote(m_ref.at[k], mpo_raw.at[k], mpo_send.at[k], mpo_sem.at[k], partner) for k in range(2)]
        for k in range(2):
            left_stage_copy(k).wait()
            for pair in range(4):
                pack_left(k, pair)
                left_send_copy(k, pair, k).start()
            right_copies[k].start()
            mpo_copies[k].start()
        pltpu.make_async_copy(slab, slab, slab_sem).wait()
        acc = jnp.zeros((8, 128), F32)
        for k in range(4):
            acc = acc + fold(slab[k])
        exchange_squares(acc)
        inverse = inverse_scale()
        scale_in[...] = inverse
        scale_copy = remote(scale_in, scale_in, scale_send, scale_sem, partner)
        scale_copy.start()
        write_out(inverse)
        scale_copy.wait_send()
        wait_squares_sent()
        wait_left_sent()
        for k in range(2):
            right_copies[k].wait_send()
            mpo_copies[k].wait_send()

    @pl.when(core == 1)
    def _():
        def prepare_left(lattice_row):
            for pair in range(4):
                pltpu.make_async_copy(
                    left_in.at[lattice_row, pair], left_in.at[lattice_row, pair], left_sem.at[lattice_row, pair]
                ).wait()
                high, low = halves(left_in[lattice_row, pair])
                left_high[:, pair * 128:pair * 128 + 128] = high
                left_low[:, pair * 128:pair * 128 + 128] = low

        def prepare_right(lattice_row):
            pltpu.make_async_copy(right_raw.at[lattice_row], right_raw.at[lattice_row], right_sem.at[lattice_row]).wait()
            turned = right_raw[lattice_row].reshape(512, 256).T
            high, low = halves(turned)
            for c in range(4):
                lanes = slice(c * 128, c * 128 + 128)
                right_parts[c, :, 0:128] = high[:, lanes]
                right_parts[c, :, 128:256] = high[:, lanes]
                right_parts[c, :, 256:384] = low[:, lanes]
            pltpu.make_async_copy(mpo_raw.at[lattice_row], mpo_raw.at[lattice_row], mpo_sem.at[lattice_row]).wait()
            turned = jnp.concatenate([mpo_raw[lattice_row, :, d, :].T for d in range(8)], axis=0)
            high, low = halves(turned)
            mpo_parts[...] = jnp.concatenate([high, high, low], axis=1)

        def first_copy(step):
            return remote(b_ref, first_in.at[col], first_send.at[step - 1], first_sem.at[col], (1, site, in_row(step)))

        pltpu.make_async_copy(b_ref, first_in.at[col], first_sem.at[col]).start()
        for step in (2, 1, 3):
            first_copy(step).start()
        for k in range(2):
            pltpu.make_async_copy(own_right(k), right_raw.at[2 + k], right_sem.at[2 + k]).start()
            pltpu.make_async_copy(m_ref.at[k], mpo_raw.at[2 + k], mpo_sem.at[2 + k]).start()
        for k in range(2):
            left_stage_copy(k).wait()
            for pair in range(4):
                pack_left(k, pair)
        prepare_right(0)
        prepare_left(0)

        def gather_copy(lattice_row, c, step):
            return remote(
                gathered.at[lattice_row, c, col], gathered.at[lattice_row, c, col],
                gather_send.at[lattice_row], gather_sem.at[lattice_row, c], (1, site, in_row(step)),
            )

        def absorb_chunk(lattice_row, c):
            @pl.when(lattice_row == 0)
            def _():
                pltpu.make_async_copy(first_in.at[c], first_in.at[c], first_sem.at[c]).wait()
                for u in range(8):
                    for r0 in (0, 8):
                        for pair in range(2):
                            lanes = slice(pair * 128, pair * 128 + 128)
                            lhs_rows[pair, pl.ds(r0 * 8 + u, 8, stride=8), :] = first_in[c, u, r0:r0 + 8, lanes]

            @pl.when(lattice_row > 0)
            def _():
                source = lattice_row - 1
                three = gathered.at[source, c, pl.ds(0, 3)]
                pltpu.make_async_copy(three, three, gather_sem.at[source, c]).wait()
                for r0 in (0, 8):
                    for pair in range(2):
                        for u_pair in range(4):
                            block = slice(u_pair * 128, u_pair * 128 + 128)
                            first = gathered[source, c, 2 * pair, r0:r0 + 8, block]
                            second = gathered[source, c, 2 * pair + 1, r0:r0 + 8, block]
                            start = r0 * 8 + 2 * u_pair
                            lhs_rows[pair, pl.ds(start, 8, stride=8), :] = pair_even(first, second)
                            lhs_rows[pair, pl.ds(start + 1, 8, stride=8), :] = pair_odd(first, second)

            high, low = halves(jnp.concatenate([lhs_rows[0], lhs_rows[1]], axis=1))
            both = dot(jnp.concatenate([high, low], axis=0), left_high[...])
            left_part = both[0:128] + both[128:256] + dot(high, left_low[...])
            for pair in range(4):
                lanes = slice(pair * 128, pair * 128 + 128)
                first = left_part[0:64, lanes]
                second = left_part[64:128, lanes]
                even = pair_even(first, second)
                odd = pair_odd(first, second)
                for k in range(8):
                    mixed_in[pair * 16:pair * 16 + 8, k * 128:k * 128 + 128] = even[k * 8:k * 8 + 8]
                    mixed_in[pair * 16 + 8:pair * 16 + 16, k * 128:k * 128 + 128] = odd[k * 8:k * 8 + 8]
            high, low = halves(mixed_in[...])
            mixed = dot(mpo_parts[...], jnp.concatenate([high, low, high], axis=0))
            for pair in range(4):
                lanes = slice(pair * 128, pair * 128 + 128)
                for k in range(8):
                    block = slice(k * 128, k * 128 + 128)
                    first = mixed[pair * 16:pair * 16 + 8, block]
                    second = mixed[pair * 16 + 8:pair * 16 + 16, block]
                    mixed_out[k * 8:k * 8 + 8, lanes] = pair_even(first, second)
                    mixed_out[64 + k * 8:64 + k * 8 + 8, lanes] = pair_odd(first, second)
            high, low = halves(mixed_out[...])
            added = dot(right_parts[c], jnp.concatenate([high, low, high], axis=0))

            @pl.when(c == 0)
            def _():
                partial[lattice_row] = added

            @pl.when(c > 0)
            def _():
                partial[lattice_row] += added

        def partial_copy(lattice_row, c, step):
            target_row = lax.rem(row + step, 4)
            rows = pl.ds(pl.multiple_of(target_row * 64 + c * 16, 16), 16)
            return remote(
                partial.at[lattice_row, rows], partial_in.at[lattice_row, c, step - 1],
                partial_send.at[lattice_row], partial_sem.at[lattice_row, c], (1, site, in_col(step)),
            )

        def reduced(lattice_row, c):
            every = partial_in.at[lattice_row, c]
            pltpu.make_async_copy(every, every, partial_sem.at[lattice_row, c]).wait()
            rows = pl.ds(pl.multiple_of(row * 64 + c * 16, 16), 16)
            total = partial[lattice_row, rows, :]
            for k in range(3):
                total = total + partial_in[lattice_row, c, k]
            return total

        def slab_out():
            return remote(gathered.at[1, col], slab, slab_send, slab_sem, (0, site, bond))

        def final_copy(c):
            return remote(gathered.at[3, c, col], slab.at[col], slab_send, slab_sem, (1, site, row * 4 + c))

        @pl.loop(0, 4)
        def _(lattice_row):
            @pl.loop(0, 4)
            def _(c):
                absorb_chunk(lattice_row, c)

            @pl.loop(0, 4)
            def _(c):
                for step in (2, 1, 3):
                    partial_copy(lattice_row, c, step).start()

            @pl.when(lattice_row < 2)
            def _():
                for pair in range(4):
                    left_send_copy(lattice_row, pair, lattice_row + 2).start()

            @pl.when(lattice_row == 2)
            def _():
                slab_out().start()

            @pl.when(lattice_row < 3)
            def _():
                prepare_right(lattice_row + 1)

                @pl.loop(0, 4)
                def _(c):
                    gathered[lattice_row, c, col] = reduced(lattice_row, c)
                    for step in (2, 1, 3):
                        gather_copy(lattice_row, c, step).start()

                prepare_left(lattice_row + 1)

        slab_out().wait_send()
        pltpu.make_async_copy(scale_in, scale_in, scale_sem).wait()
        inverse = scale_in[0:1, 0:1]
        acc = jnp.zeros((8, 128), F32)
        for c in range(4):
            total = reduced(3, c) * inverse
            acc = acc + fold(total)

            @pl.when(col == c)
            def _():
                slab[c] = total

            @pl.when(col != c)
            def _():
                gathered[3, c, col] = total
                final_copy(c).start()

        exchange_squares(acc)
        three = slab.at[pl.ds(0, 3)]
        pltpu.make_async_copy(three, three, slab_sem).wait()
        write_out(inverse_scale())

        pltpu.make_async_copy(three, three, slab_send).wait()
        wait_squares_sent()
        wait_left_sent()
        for step in (1, 2, 3):
            first_copy(step).wait_send()
        for k in range(4):
            sent = partial.at[k, pl.ds(0, 192)]
            pltpu.make_async_copy(sent, sent, partial_send.at[k]).wait()
        for k in range(3):
            sent = gathered.at[k, pl.ds(0, 3)]
            pltpu.make_async_copy(sent, sent, gather_send.at[k]).wait()


def body(boundary_in, mpo, proj):
    b = jnp.transpose(boundary_in[0, 0], (1, 2, 0))
    m = mpo.reshape(2, 64, 8, 8)
    p = proj.reshape(2, 256, 8, 256)
    dma = pltpu.SemaphoreType.DMA
    out = pl.pallas_call(
        kernel,
        out_shape=jax.ShapeDtypeStruct((8, 16, 256), F32),
        in_specs=[pl.BlockSpec(memory_space=pltpu.HBM)] * 3,
        out_specs=pl.BlockSpec(memory_space=pltpu.VMEM),
        scratch_shapes=[
            pltpu.VMEM((4, 8, 16, 256), F32),
            pltpu.VMEM((4, 4, 4, 16, 512), F32),
            pltpu.VMEM((4, 4, 3, 16, 512), F32),
            pltpu.VMEM((4, 256, 512), F32),
            pltpu.VMEM((4, 16, 512), F32),
            pltpu.VMEM((16, 8, 128), F32),
            pltpu.VMEM((8, 128), F32),
            pltpu.VMEM((8, 128), F32),
            pltpu.VMEM((2, 256, 8, 128), F32),
            pltpu.VMEM((2, 4, 256, 128), F32),
            pltpu.VMEM((4, 4, 256, 128), F32),
            pltpu.VMEM((4, 64, 8, 256), F32),
            pltpu.VMEM((4, 64, 8, 8), F32),
            pltpu.VMEM((256, 512), BF16),
            pltpu.VMEM((256, 512), BF16),
            pltpu.VMEM((4, 256, 384), BF16),
            pltpu.VMEM((64, 192), BF16),
            pltpu.VMEM((2, 128, 128), F32),
            pltpu.VMEM((64, 1024), F32),
            pltpu.VMEM((128, 512), F32),
            dma((4,)), dma((3, 4)), dma((4, 4)), dma, dma, dma,
            dma((4, 4)), dma((4,)), dma((4,)), dma((2,)),
            dma((3,)), dma((3,)), dma((4,)), dma, dma, dma,
            dma((2,)), dma((2,)), dma((2,)),
        ],
        compiler_params=pltpu.CompilerParams(
            collective_id=0, has_side_effects=True, vmem_limit_bytes=61 * 1024 * 1024
        ),
        name="absorb",
    )(b, p, m)
    return jnp.transpose(out, (2, 0, 1))[None, None, None]


def solution(mesh):
    return jax.shard_map(
        body,
        mesh=mesh,
        in_specs=(
            P(None, "sites", None, None, "bond"),
            P("rows", "sites", None, None, None, None),
            P("rows", "sites", None, None, None),
        ),
        out_specs=P("rows", None, "sites", None, None, "bond"),
        check_vma=False,
    )
```

time: 552 us -> 66.8 us (0.12); the launches traced: 544 us -> 66.7 us
  waiting for transfers between devices: 411 us -> 0 us
  Pallas kernels: 0 us -> 65.1 us
  blocking collectives: 63 us -> 0 us
  matrix products: 27.2 us -> 0 us
  local copies, waits for them, and re-layouts: 18.3 us -> 1.57 us
  between operations: 14.6 us -> 0.01 us
    reduce_scatter x4 -> x0, waiting for transfers between devices: 309 us -> none  [body(): lax.psum_scatter(partial_value, 'bond', scatter_dimension=3, tiled=True)]
    ppermute x2 -> x0, waiting for transfers between devices: 102 us -> none  [the longest x1 91.8 us: from_behind(): lax.ppermute(shard, axis, [(i, (i + by) % size) for i in range(size)])]
    pallas_call x0 -> x1, Pallas kernels: none -> 65.1 us  [body(): pl.pallas_call(kernel, out_shape=jax.ShapeDtypeStruct((8, 16, 256), F32),...]
    psum x2 -> x0, blocking collectives: 63 us -> none  [body(): norm_total = lax.psum(square_sum, 'bond')]
    dot_general x12 -> x0, matrix products: 27.2 us -> none  [the longest x4 11.5 us: left_mix(): jnp.einsum('alx,taub->tlxub', left_proj, boundary, precision=precise)]
    dot_general x4 -> x0, local copies, waits for them, and re-layouts: 9.14 us -> none  [body(): jnp.einsum('txdbr,bry->txdy', mixed_rows, right_rows, precision=precise)]
  transfers between devices with their start and end apart: 6 -> 0, of which waited for: 6 -> 0; matrix products, arithmetic and copies ran while one was open for 1% -> 0% of each run, Pallas kernels for 0% -> 0%
where the time goes in v1:
time: 66.8 us; the launch traced here: 66.7 us
  Pallas kernels  65.1 us (97%)
  local copies, waits for them, and re-layouts  1.57 us (2%)
    pallas_call x1, Pallas kernels, body(): pl.pallas_call(kernel, out_shape=jax.ShapeDtypeStruct((8, 16, 256), F32),...  65.1 us
    unnamed x1, local copies, waits for them, and re-layouts  1.57 us

profile of v1, /device:TPU:1, one launch (start us, length us, event | category | flops | bytes accessed | tf_op | source)
XLA Modules:
  0.0 66.7 jit_solution(8291589009877608190)
XLA Ops:
  0.0 65.1 %absorb.1 = f32[8,16,256]{2,1,0:T(8,128)} custom-call(f32[8,16,256]{2,1,0:T(8,128)} %bitcast.11, f32[2,256,8,256]{3,2,1,0:T(8,128)} %bitcast.8, f32[2,64,8,8]{3,2,1,0:T(8,128)} %bitcast.9), custom_call_target="tpu_custom_call" | custom-call | tf_op jit(solution)/shard_map/absorb/pallas_call | solution.py:371
  65.2 1.6 %copy.5 = f32[1,1,1,256,8,16]{3,5,4,2,1,0:T(8,128)} copy(f32[1,1,1,256,8,16]{3,5,4,2,1,0:T(8,128)} %bitcast.10) | data formatting | bytes 262144

commit v2 on v1

--- a/solution.py
+++ b/solution.py
@@ -35,12 +35,13 @@
 
 def kernel(
     b_ref, p_ref, m_ref, out_ref,
-    first_in, gathered, partial_in, partial, slab, squares, own_square, scale_in,
+    first_raw, first_packed, first_in, first_left, first_out, turned_rows, gathered, partial_in, partial, slab, squares, own_square, scale_in,
     left_stage, left_packed, left_in, right_raw, mpo_raw,
-    left_high, left_low, right_parts, mpo_parts, lhs_rows, mixed_in, mixed_out,
-    first_sem, gather_sem, partial_sem, slab_sem, square_sem, scale_sem,
+    left_high, left_low, turned_high, turned_low, right_parts, mpo_parts, lhs_rows, mixed_in, mixed_out,
+    raw_sem, first_sem, first_left_sem, first_left_send, open_sem,
+    gather_sem, partial_sem, slab_sem, square_sem, scale_sem,
     left_sem, right_sem, mpo_sem, stage_sem,
-    first_send, gather_send, partial_send, slab_send, square_send, scale_send,
+    ready_sem, first_send, gather_send, partial_send, slab_send, square_send, scale_send,
     left_send, right_send, mpo_send,
 ):
     core = lax.axis_index("rows")
@@ -63,20 +64,30 @@
         )
 
     def left_stage_copy(k):
-        block = pl.ds(pl.multiple_of((col // 2) * 128, 128), 128)
+        part = jnp.where((core == 0) & (k == 0), row, col)
+        block = pl.ds(pl.multiple_of((part // 2) * 128, 128), 128)
         return pltpu.make_async_copy(p_ref.at[k, :, :, block], left_stage.at[k], stage_sem.at[k])
 
     def own_right(k):
         return p_ref.at[k, pl.ds(row * 64, 64)]
 
     barrier = pltpu.get_barrier_semaphore()
-    peers = [(core, site, lax.rem(bond + k, 16)) for k in range(1, 16)]
-    peers += [(1 - core, site, bond), (0, next_site, bond), (1, next_site, bond), (0, prev_site, bond), (1, prev_site, bond)]
     for k in range(2):
         left_stage_copy(k).start()
-    for peer in peers:
-        pl.semaphore_signal(barrier, inc=1, device_id=peer, device_id_type=MESH)
-    pl.semaphore_wait(barrier, len(peers))
+
+    def greet(device):
+        pl.semaphore_signal(barrier, inc=1, device_id=device, device_id_type=MESH)
+
+    @pl.when(core == 0)
+    def _():
+        greet((1, site, bond))
+        pl.semaphore_wait(barrier, 1)
+
+    @pl.when(core == 1)
+    def _():
+        greet((0, prev_site, bond))
+        for step in range(1, 16):
+            greet((1, site, lax.rem(bond + step, 16)))
 
     def left_send_copy(k, pair, lattice_row):
         return remote(
@@ -87,7 +98,7 @@
     def pack_left(k, pair):
         first = left_stage[k, :, 2 * pair, :]
         second = left_stage[k, :, 2 * pair + 1, :]
-        half = lax.rem(col, 2)
+        half = lax.rem(jnp.where((core == 0) & (k == 0), row, col), 2)
 
         @pl.when(half == 0)
         def _():
@@ -142,15 +153,32 @@
     @pl.when(core == 0)
     def _():
         partner = (1, site, bond)
-        right_copies = [remote(own_right(k), right_raw.at[k], right_send.at[k], right_sem.at[k], partner) for k in range(2)]
+        own_left = p_ref.at[0, pl.ds(col * 64, 64)]
+        for k in range(2):
+            remote(
+                own_left.at[:, :, pl.ds(k * 128, 128)], first_left.at[k], first_left_send, first_left_sem.at[k],
+                (1, next_site, bond),
+            ).start()
+        first_right = [
+            remote(left_packed.at[0, pair], left_in.at[0, pair], left_send.at[0], left_sem.at[0, pair], partner)
+            for pair in range(4)
+        ]
+        right_copy = remote(own_right(1), right_raw.at[1], right_send, right_sem.at[1], partner)
         mpo_copies = [remote(m_ref.at[k], mpo_raw.at[k], mpo_send.at[k], mpo_sem.at[k], partner) for k in range(2)]
+        left_stage_copy(0).wait()
+        for pair in range(4):
+            pack_left(0, pair)
+        pl.semaphore_wait(open_sem, 1)
+        pl.semaphore_signal(ready_sem, inc=1, device_id=partner, device_id_type=MESH)
+        for pair in range(4):
+            first_right[pair].start()
         for k in range(2):
-            left_stage_copy(k).wait()
-            for pair in range(4):
-                pack_left(k, pair)
-                left_send_copy(k, pair, k).start()
-            right_copies[k].start()
             mpo_copies[k].start()
+        left_stage_copy(1).wait()
+        for pair in range(4):
+            pack_left(1, pair)
+            left_send_copy(1, pair, 1).start()
+        right_copy.start()
         pltpu.make_async_copy(slab, slab, slab_sem).wait()
         acc = jnp.zeros((8, 128), F32)
         for k in range(4):
@@ -164,9 +192,10 @@
         scale_copy.wait_send()
         wait_squares_sent()
         wait_left_sent()
+        right_copy.wait_send()
         for k in range(2):
-            right_copies[k].wait_send()
             mpo_copies[k].wait_send()
+        pltpu.make_async_copy(first_left, first_left, first_left_send).wait()
 
     @pl.when(core == 1)
     def _():
@@ -194,55 +223,33 @@
             mpo_parts[...] = jnp.concatenate([high, high, low], axis=1)
 
         def first_copy(step):
-            return remote(b_ref, first_in.at[col], first_send.at[step - 1], first_sem.at[col], (1, site, in_row(step)))
-
-        pltpu.make_async_copy(b_ref, first_in.at[col], first_sem.at[col]).start()
-        for step in (2, 1, 3):
-            first_copy(step).start()
+            target = lax.rem(bond + step, 16)
+            return remote(
+                first_packed.at[lax.rem(target, 4)], first_in.at[bond], first_send, first_sem, (1, site, target)
+            )
+
+        raw_copy = pltpu.make_async_copy(b_ref, first_raw, raw_sem)
+        raw_copy.start()
         for k in range(2):
             pltpu.make_async_copy(own_right(k), right_raw.at[2 + k], right_sem.at[2 + k]).start()
             pltpu.make_async_copy(m_ref.at[k], mpo_raw.at[2 + k], mpo_sem.at[2 + k]).start()
-        for k in range(2):
-            left_stage_copy(k).wait()
-            for pair in range(4):
-                pack_left(k, pair)
-        prepare_right(0)
-        prepare_left(0)
-
-        def gather_copy(lattice_row, c, step):
-            return remote(
-                gathered.at[lattice_row, c, col], gathered.at[lattice_row, c, col],
-                gather_send.at[lattice_row], gather_sem.at[lattice_row, c], (1, site, in_row(step)),
-            )
-
-        def absorb_chunk(lattice_row, c):
-            @pl.when(lattice_row == 0)
-            def _():
-                pltpu.make_async_copy(first_in.at[c], first_in.at[c], first_sem.at[c]).wait()
-                for u in range(8):
-                    for r0 in (0, 8):
-                        for pair in range(2):
-                            lanes = slice(pair * 128, pair * 128 + 128)
-                            lhs_rows[pair, pl.ds(r0 * 8 + u, 8, stride=8), :] = first_in[c, u, r0:r0 + 8, lanes]
-
-            @pl.when(lattice_row > 0)
-            def _():
-                source = lattice_row - 1
-                three = gathered.at[source, c, pl.ds(0, 3)]
-                pltpu.make_async_copy(three, three, gather_sem.at[source, c]).wait()
-                for r0 in (0, 8):
-                    for pair in range(2):
-                        for u_pair in range(4):
-                            block = slice(u_pair * 128, u_pair * 128 + 128)
-                            first = gathered[source, c, 2 * pair, r0:r0 + 8, block]
-                            second = gathered[source, c, 2 * pair + 1, r0:r0 + 8, block]
-                            start = r0 * 8 + 2 * u_pair
-                            lhs_rows[pair, pl.ds(start, 8, stride=8), :] = pair_even(first, second)
-                            lhs_rows[pair, pl.ds(start + 1, 8, stride=8), :] = pair_odd(first, second)
-
-            high, low = halves(jnp.concatenate([lhs_rows[0], lhs_rows[1]], axis=1))
-            both = dot(jnp.concatenate([high, low], axis=0), left_high[...])
-            left_part = both[0:128] + both[128:256] + dot(high, left_low[...])
+        raw_copy.wait()
+        for block in range(2):
+            for u_pair in range(4):
+                first = first_raw[2 * u_pair, :, block * 128:block * 128 + 128]
+                second = first_raw[2 * u_pair + 1, :, block * 128:block * 128 + 128]
+                lanes = slice(u_pair * 128, u_pair * 128 + 128)
+                first_packed[2 * block, :, lanes] = pair_even(first, second)
+                first_packed[2 * block + 1, :, lanes] = pair_odd(first, second)
+        pltpu.make_async_copy(first_packed.at[col], first_in.at[bond], first_sem).start()
+        pl.semaphore_wait(barrier, 16)
+        pl.semaphore_signal(open_sem, inc=1, device_id=(0, site, bond), device_id_type=MESH)
+        for step in (10, 6, 2, 8, 9, 7, 5, 11, 14, 3, 13, 15, 1, 4, 12):
+            first_copy(step).start()
+
+        def mix(rows_high, rows_low, c):
+            both = dot(jnp.concatenate([rows_high, rows_low], axis=0), left_high[...])
+            left_part = both[0:128] + both[128:256] + dot(rows_high, left_low[...])
             for pair in range(4):
                 lanes = slice(pair * 128, pair * 128 + 128)
                 first = left_part[0:64, lanes]
@@ -250,9 +257,10 @@
                 even = pair_even(first, second)
                 odd = pair_odd(first, second)
                 for k in range(8):
-                    mixed_in[pair * 16:pair * 16 + 8, k * 128:k * 128 + 128] = even[k * 8:k * 8 + 8]
-                    mixed_in[pair * 16 + 8:pair * 16 + 16, k * 128:k * 128 + 128] = odd[k * 8:k * 8 + 8]
-            high, low = halves(mixed_in[...])
+                    block = slice(k * 128, k * 128 + 128)
+                    mixed_in[c, pair * 16:pair * 16 + 8, block] = even[k * 8:k * 8 + 8]
+                    mixed_in[c, pair * 16 + 8:pair * 16 + 16, block] = odd[k * 8:k * 8 + 8]
+            high, low = halves(mixed_in[c])
             mixed = dot(mpo_parts[...], jnp.concatenate([high, low, high], axis=0))
             for pair in range(4):
                 lanes = slice(pair * 128, pair * 128 + 128)
@@ -260,31 +268,104 @@
                     block = slice(k * 128, k * 128 + 128)
                     first = mixed[pair * 16:pair * 16 + 8, block]
                     second = mixed[pair * 16 + 8:pair * 16 + 16, block]
-                    mixed_out[k * 8:k * 8 + 8, lanes] = pair_even(first, second)
-                    mixed_out[64 + k * 8:64 + k * 8 + 8, lanes] = pair_odd(first, second)
-            high, low = halves(mixed_out[...])
+                    mixed_out[c, k * 8:k * 8 + 8, lanes] = pair_even(first, second)
+                    mixed_out[c, 64 + k * 8:64 + k * 8 + 8, lanes] = pair_odd(first, second)
+
+        def close(lattice_row, c):
+            high, low = halves(mixed_out[c])
             added = dot(right_parts[c], jnp.concatenate([high, low, high], axis=0))
-
-            @pl.when(c == 0)
-            def _():
+            if c == 0:
                 partial[lattice_row] = added
-
-            @pl.when(c > 0)
-            def _():
+            else:
                 partial[lattice_row] += added
 
+        def gather_copy(lattice_row, c, step):
+            return remote(
+                gathered.at[lattice_row, c, col], gathered.at[lattice_row, c, col],
+                gather_send.at[lattice_row], gather_sem.at[lattice_row, c], (1, site, in_row(step)),
+            )
+
+        def first_row():
+            for pair in range(4):
+                arrived = left_in.at[0, pair]
+                pltpu.make_async_copy(arrived, arrived, left_sem.at[0, pair]).wait()
+                turned = left_in[0, pair].T
+                for k in range(2):
+                    for block in range(2):
+                        turned_rows[block, pl.ds(2 * pair + k, 64, stride=8), :] = (
+                            turned[k * 64:k * 64 + 64, block * 128:block * 128 + 128]
+                        )
+            high, low = halves(jnp.concatenate([turned_rows[0], turned_rows[1]], axis=1))
+            turned_high[...] = high
+            turned_low[...] = low
+            pltpu.make_async_copy(mpo_raw.at[0], mpo_raw.at[0], mpo_sem.at[0]).wait()
+            turned = mpo_raw[0].reshape(8, 8, 8, 8)
+            turned = jnp.concatenate([turned[:, u].reshape(64, 8) for u in range(8)], axis=1)
+            high, low = halves(turned)
+            mpo_parts[...] = jnp.concatenate([high, high, low], axis=1)
+            for k in range(2):
+                left_stage_copy(k).wait()
+                for pair in range(4):
+                    pack_left(k, pair)
+            pltpu.make_async_copy(first_in, first_in, first_sem).wait()
+            high, low = halves(first_in[...].reshape(256, 512))
+            left_high[...] = high
+            left_low[...] = low
+            for c in range(4):
+                rows = slice(c * 128, c * 128 + 128)
+                mix(turned_high[rows, :], turned_low[rows, :], c)
+            for block in range(2):
+                pltpu.make_async_copy(first_left.at[block], first_left.at[block], first_left_sem.at[block]).wait()
+                right = jnp.concatenate([first_left[block, :, l, :] for l in range(8)], axis=0)
+                right_high, right_low = halves(right)
+                high, low = halves(mixed_out[...].reshape(512, 512))
+                both = dot(jnp.concatenate([high, low], axis=0), right_high)
+                first_out[block] = both[0:512] + both[512:1024] + dot(high, right_low)
+                for d_pair in range(4):
+                    first = first_out[block, pl.ds(2 * d_pair, 64, stride=8), :]
+                    second = first_out[block, pl.ds(2 * d_pair + 1, 64, stride=8), :]
+                    lanes = slice(d_pair * 128, d_pair * 128 + 128)
+                    partial[0, block * 128:block * 128 + 64, lanes] = pair_even(first, second)
+                    partial[0, block * 128 + 64:block * 128 + 128, lanes] = pair_odd(first, second)
+
+        def place_rows(lattice_row, c):
+            source = lattice_row - 1
+            three = gathered.at[source, c, pl.ds(0, 3)]
+            pltpu.make_async_copy(three, three, gather_sem.at[source, c]).wait()
+            for r0 in (0, 8):
+                for pair in range(2):
+                    for u_pair in range(4):
+                        block = slice(u_pair * 128, u_pair * 128 + 128)
+                        first = gathered[source, c, 2 * pair, r0:r0 + 8, block]
+                        second = gathered[source, c, 2 * pair + 1, r0:r0 + 8, block]
+                        start = r0 * 8 + 2 * u_pair
+                        lhs_rows[pair, pl.ds(start, 8, stride=8), :] = pair_even(first, second)
+                        lhs_rows[pair, pl.ds(start + 1, 8, stride=8), :] = pair_odd(first, second)
+            return halves(jnp.concatenate([lhs_rows[0], lhs_rows[1]], axis=1))
+
+        def later_row(lattice_row):
+            for c in range(4):
+                high, low = place_rows(lattice_row, c)
+                mix(high, low, c)
+                if c > 0:
+                    close(lattice_row, c - 1)
+            close(lattice_row, 3)
+
         def partial_copy(lattice_row, c, step):
-            target_row = lax.rem(row + step, 4)
-            rows = pl.ds(pl.multiple_of(target_row * 64 + c * 16, 16), 16)
+            is_first = lattice_row == 0
+            target = lax.rem(jnp.where(is_first, col, row) + step, 4)
+            rows = pl.ds(pl.multiple_of(target * 64 + c * 16, 16), 16)
+            device = jnp.where(is_first, in_row(step), in_col(step))
             return remote(
                 partial.at[lattice_row, rows], partial_in.at[lattice_row, c, step - 1],
-                partial_send.at[lattice_row], partial_sem.at[lattice_row, c], (1, site, in_col(step)),
+                partial_send.at[lattice_row], partial_sem.at[lattice_row, c], (1, site, device),
             )
 
         def reduced(lattice_row, c):
             every = partial_in.at[lattice_row, c]
             pltpu.make_async_copy(every, every, partial_sem.at[lattice_row, c]).wait()
-            rows = pl.ds(pl.multiple_of(row * 64 + c * 16, 16), 16)
+            own = jnp.where(lattice_row == 0, col, row)
+            rows = pl.ds(pl.multiple_of(own * 64 + c * 16, 16), 16)
             total = partial[lattice_row, rows, :]
             for k in range(3):
                 total = total + partial_in[lattice_row, c, k]
@@ -298,14 +379,22 @@
 
         @pl.loop(0, 4)
         def _(lattice_row):
-            @pl.loop(0, 4)
-            def _(c):
-                absorb_chunk(lattice_row, c)
+            @pl.when(lattice_row == 0)
+            def _():
+                first_row()
+
+            @pl.when(lattice_row > 0)
+            def _():
+                later_row(lattice_row)
 
             @pl.loop(0, 4)
             def _(c):
                 for step in (2, 1, 3):
                     partial_copy(lattice_row, c, step).start()
+
+            @pl.when(lattice_row == 0)
+            def _():
+                pl.semaphore_wait(ready_sem, 1)
 
             @pl.when(lattice_row < 2)
             def _():
@@ -353,8 +442,7 @@
         pltpu.make_async_copy(three, three, slab_send).wait()
         wait_squares_sent()
         wait_left_sent()
-        for step in (1, 2, 3):
-            first_copy(step).wait_send()
+        pltpu.make_async_copy(first_in.at[pl.ds(0, 15)], first_in.at[pl.ds(0, 15)], first_send).wait()
         for k in range(4):
             sent = partial.at[k, pl.ds(0, 192)]
             pltpu.make_async_copy(sent, sent, partial_send.at[k]).wait()
@@ -367,6 +455,7 @@
     b = jnp.transpose(boundary_in[0, 0], (1, 2, 0))
     m = mpo.reshape(2, 64, 8, 8)
     p = proj.reshape(2, 256, 8, 256)
+    b, m, p = (pltpu.with_memory_space_constraint(v, pltpu.HBM) for v in (b, m, p))
     dma = pltpu.SemaphoreType.DMA
     out = pl.pallas_call(
         kernel,
@@ -374,7 +463,12 @@
         in_specs=[pl.BlockSpec(memory_space=pltpu.HBM)] * 3,
         out_specs=pl.BlockSpec(memory_space=pltpu.VMEM),
         scratch_shapes=[
-            pltpu.VMEM((4, 8, 16, 256), F32),
+            pltpu.VMEM((8, 16, 256), F32),
+            pltpu.VMEM((4, 16, 512), F32),
+            pltpu.VMEM((16, 16, 512), F32),
+            pltpu.VMEM((2, 64, 8, 128), F32),
+            pltpu.VMEM((2, 512, 128), F32),
+            pltpu.VMEM((2, 512, 128), F32),
             pltpu.VMEM((4, 4, 4, 16, 512), F32),
             pltpu.VMEM((4, 4, 3, 16, 512), F32),
             pltpu.VMEM((4, 256, 512), F32),
@@ -389,18 +483,22 @@
             pltpu.VMEM((4, 64, 8, 8), F32),
             pltpu.VMEM((256, 512), BF16),
             pltpu.VMEM((256, 512), BF16),
+            pltpu.VMEM((512, 256), BF16),
+            pltpu.VMEM((512, 256), BF16),
             pltpu.VMEM((4, 256, 384), BF16),
             pltpu.VMEM((64, 192), BF16),
             pltpu.VMEM((2, 128, 128), F32),
-            pltpu.VMEM((64, 1024), F32),
-            pltpu.VMEM((128, 512), F32),
-            dma((4,)), dma((3, 4)), dma((4, 4)), dma, dma, dma,
+            pltpu.VMEM((4, 64, 1024), F32),
+            pltpu.VMEM((4, 128, 512), F32),
+            dma, dma, dma((2,)), dma, pltpu.SemaphoreType.REGULAR,
+            dma((3, 4)), dma((4, 4)), dma, dma, dma,
             dma((4, 4)), dma((4,)), dma((4,)), dma((2,)),
-            dma((3,)), dma((3,)), dma((4,)), dma, dma, dma,
-            dma((2,)), dma((2,)), dma((2,)),
+            pltpu.SemaphoreType.REGULAR,
+            dma, dma((3,)), dma((4,)), dma, dma, dma,
+            dma((2,)), dma, dma((2,)),
         ],
         compiler_params=pltpu.CompilerParams(
-            collective_id=0, has_side_effects=True, vmem_limit_bytes=61 * 1024 * 1024
+            collective_id=0, has_side_effects=True, vmem_limit_bytes=40 * 1024 * 1024
         ),
         name="absorb",
     )(b, p, m)

time: 66.8 us -> 56.1 us (0.84)
  Pallas kernels: 65.1 us -> 55.4 us
  local copies, waits for them, and re-layouts: 1.57 us -> 0.66 us
    pallas_call x1, Pallas kernels: 65.1 us -> 55.4 us  [body(): pl.pallas_call(kernel, out_shape=jax.ShapeDtypeStruct((8, 16, 256), F32),...]
    unnamed x1, local copies, waits for them, and re-layouts: 1.57 us -> 0.66 us
where the time goes in v2:
time: 56.1 us; the launch traced here: 56 us
  Pallas kernels  55.4 us (99%)
  local copies, waits for them, and re-layouts  0.66 us (1%)
    pallas_call x1, Pallas kernels, body(): pl.pallas_call(kernel, out_shape=jax.ShapeDtypeStruct((8, 16, 256), F32),...  55.4 us

profile of v2, /device:TPU:1, one launch (start us, length us, event | category | flops | bytes accessed | tf_op | source)
XLA Modules:
  0.0 56.0 jit_solution(3213172563181491827)
XLA Ops:
  0.0 55.4 %absorb.1 = f32[8,16,256]{2,1,0:T(8,128)S(1)} custom-call(f32[8,16,256]{2,1,0:T(8,128)} %bitcast.11, f32[2,256,8,256]{3,2,1,0:T(8,128)} %bitcast.9, f32[2,64,8,8]{3,2,1,0:T(8,128)} %bitcast.10), custom_call_target="tpu_custom_call" | custom-call | tf_op jit(solution)/shard_map/absorb/pallas_call | solution.py:460
  55.4 0.7 %copy.5 = f32[1,1,1,256,8,16]{3,5,4,2,1,0:T(8,128)} copy(f32[1,1,1,256,8,16]{3,5,4,2,1,0:T(8,128)S(1)} %bitcast.8) | data formatting | bytes 262144

commit v3 on v2

--- a/solution.py
+++ b/solution.py
@@ -38,7 +38,7 @@
     first_raw, first_packed, first_in, first_left, first_out, turned_rows, gathered, partial_in, partial, slab, squares, own_square, scale_in,
     left_stage, left_packed, left_in, right_raw, mpo_raw,
     left_high, left_low, turned_high, turned_low, right_parts, mpo_parts, lhs_rows, mixed_in, mixed_out,
-    raw_sem, first_sem, first_left_sem, first_left_send, open_sem,
+    raw_sem, first_sem, first_left_sem, first_left_send, lead_sem, lead_send, tail_sem, open_sem,
     gather_sem, partial_sem, slab_sem, square_sem, scale_sem,
     left_sem, right_sem, mpo_sem, stage_sem,
     ready_sem, first_send, gather_send, partial_send, slab_send, square_send, scale_send,
@@ -108,16 +108,19 @@
         def _():
             left_packed[k, pair] = pair_odd(first, second)
 
-    def square_copy(step):
-        return remote(
-            own_square, squares.at[bond], square_send, square_sem, (core, site, lax.rem(bond + step, 16))
-        )
+    far_first = [(2, 2), (2, 1), (2, 3), (1, 2), (3, 2), (1, 1), (1, 3), (3, 1), (3, 3), (2, 0), (0, 2), (1, 0), (3, 0), (0, 1), (0, 3)]
+
+    def other(offset):
+        return lax.rem(row + offset[0], 4) * 4 + lax.rem(col + offset[1], 4)
+
+    def square_copy(offset):
+        return remote(own_square, squares.at[bond], square_send, square_sem, (core, site, other(offset)))
 
     def exchange_squares(value):
         own_square[...] = value
         squares[bond] = value
-        for step in range(1, 16):
-            square_copy(step).start()
+        for offset in far_first:
+            square_copy(offset).start()
 
     def inverse_scale():
         pltpu.make_async_copy(squares.at[pl.ds(0, 15)], squares.at[pl.ds(0, 15)], square_sem).wait()
@@ -134,14 +137,18 @@
         return acc
 
     def write_out(inverse):
+        pieces = []
         for r0 in (0, 8):
             for pair in range(2):
                 for d_pair in range(4):
                     first = slab[2 * pair, r0:r0 + 8, d_pair * 128:d_pair * 128 + 128]
                     second = slab[2 * pair + 1, r0:r0 + 8, d_pair * 128:d_pair * 128 + 128]
                     lanes = slice(pair * 128, pair * 128 + 128)
-                    out_ref[2 * d_pair, r0:r0 + 8, lanes] = pair_even(first, second) * inverse
-                    out_ref[2 * d_pair + 1, r0:r0 + 8, lanes] = pair_odd(first, second) * inverse
+                    pieces.append((2 * d_pair, r0, lanes, pair_even(first, second)))
+                    pieces.append((2 * d_pair + 1, r0, lanes, pair_odd(first, second)))
+        scale = inverse()
+        for d, r0, lanes, value in pieces:
+            out_ref[d, r0:r0 + 8, lanes] = value * scale
 
     def wait_squares_sent():
         pltpu.make_async_copy(squares.at[pl.ds(0, 15)], squares.at[pl.ds(0, 15)], square_send).wait()
@@ -153,12 +160,16 @@
     @pl.when(core == 0)
     def _():
         partner = (1, site, bond)
-        own_left = p_ref.at[0, pl.ds(col * 64, 64)]
-        for k in range(2):
-            remote(
-                own_left.at[:, :, pl.ds(k * 128, 128)], first_left.at[k], first_left_send, first_left_sem.at[k],
-                (1, next_site, bond),
-            ).start()
+        for k in range(3):
+            quarter = lax.rem(row + k, 4)
+            lanes = pl.ds(pl.multiple_of((quarter // 2) * 128, 128), 128)
+            size = 16 if k == 0 else 32
+            for start in range(0, 32, size):
+                rows = pl.ds(col * 64 + lax.rem(quarter, 2) * 32 + start, size)
+                remote(
+                    p_ref.at[0, rows, :, lanes], first_left.at[quarter, pl.ds(start, size)], first_left_send,
+                    lead_sem.at[start // 16] if k == 0 else first_left_sem, (1, next_site, bond),
+                ).start()
         first_right = [
             remote(left_packed.at[0, pair], left_in.at[0, pair], left_send.at[0], left_sem.at[0, pair], partner)
             for pair in range(4)
@@ -188,14 +199,15 @@
         scale_in[...] = inverse
         scale_copy = remote(scale_in, scale_in, scale_send, scale_sem, partner)
         scale_copy.start()
-        write_out(inverse)
+        write_out(lambda: inverse)
         scale_copy.wait_send()
         wait_squares_sent()
         wait_left_sent()
         right_copy.wait_send()
         for k in range(2):
             mpo_copies[k].wait_send()
-        pltpu.make_async_copy(first_left, first_left, first_left_send).wait()
+        sent = first_left.at[pl.ds(0, 3)]
+        pltpu.make_async_copy(sent, sent, first_left_send).wait()
 
     @pl.when(core == 1)
     def _():
@@ -211,6 +223,8 @@
         def prepare_right(lattice_row):
             pltpu.make_async_copy(right_raw.at[lattice_row], right_raw.at[lattice_row], right_sem.at[lattice_row]).wait()
             turned = right_raw[lattice_row].reshape(512, 256).T
+            starts = [target * 64 + piece * 8 for piece in range(8) for target in range(4)]
+            turned = jnp.concatenate([turned[start:start + 8] for start in starts], axis=0)
             high, low = halves(turned)
             for c in range(4):
                 lanes = slice(c * 128, c * 128 + 128)
@@ -222,8 +236,8 @@
             high, low = halves(turned)
             mpo_parts[...] = jnp.concatenate([high, high, low], axis=1)
 
-        def first_copy(step):
-            target = lax.rem(bond + step, 16)
+        def first_copy(offset):
+            target = other(offset)
             return remote(
                 first_packed.at[lax.rem(target, 4)], first_in.at[bond], first_send, first_sem, (1, site, target)
             )
@@ -244,8 +258,8 @@
         pltpu.make_async_copy(first_packed.at[col], first_in.at[bond], first_sem).start()
         pl.semaphore_wait(barrier, 16)
         pl.semaphore_signal(open_sem, inc=1, device_id=(0, site, bond), device_id_type=MESH)
-        for step in (10, 6, 2, 8, 9, 7, 5, 11, 14, 3, 13, 15, 1, 4, 12):
-            first_copy(step).start()
+        for offset in far_first:
+            first_copy(offset).start()
 
         def mix(rows_high, rows_low, c):
             both = dot(jnp.concatenate([rows_high, rows_low], axis=0), left_high[...])
@@ -271,19 +285,24 @@
                     mixed_out[c, k * 8:k * 8 + 8, lanes] = pair_even(first, second)
                     mixed_out[c, 64 + k * 8:64 + k * 8 + 8, lanes] = pair_odd(first, second)
 
-        def close(lattice_row, c):
+        def close(lattice_row, c, start=0, size=256):
             high, low = halves(mixed_out[c])
-            added = dot(right_parts[c], jnp.concatenate([high, low, high], axis=0))
+            rows = slice(start, start + size)
+            added = dot(right_parts[c, rows, :], jnp.concatenate([high, low, high], axis=0))
             if c == 0:
-                partial[lattice_row] = added
+                partial[lattice_row, rows, :] = added
             else:
-                partial[lattice_row] += added
+                partial[lattice_row, rows, :] += added
 
         def gather_copy(lattice_row, c, step):
+            piece = gathered.at[lattice_row, c // 2, col, pl.ds(pl.multiple_of(lax.rem(c, 2) * 8, 8), 8)]
             return remote(
-                gathered.at[lattice_row, c, col], gathered.at[lattice_row, c, col],
-                gather_send.at[lattice_row], gather_sem.at[lattice_row, c], (1, site, in_row(step)),
+                piece, piece, gather_send.at[lattice_row], gather_sem.at[lattice_row, c // 2], (1, site, in_row(step))
             )
+
+        def pass_on(k):
+            lead = first_left.at[row, pl.ds(k * 16, 16)]
+            return remote(lead, lead, lead_send, tail_sem, (1, site, in_col(1)))
 
         def first_row():
             for pair in range(4):
@@ -307,6 +326,10 @@
                 left_stage_copy(k).wait()
                 for pair in range(4):
                     pack_left(k, pair)
+            for k in range(2):
+                lead = first_left.at[row, pl.ds(k * 16, 16)]
+                pltpu.make_async_copy(lead, lead, lead_sem.at[k]).wait()
+                pass_on(k).start()
             pltpu.make_async_copy(first_in, first_in, first_sem).wait()
             high, low = halves(first_in[...].reshape(256, 512))
             left_high[...] = high
@@ -314,9 +337,12 @@
             for c in range(4):
                 rows = slice(c * 128, c * 128 + 128)
                 mix(turned_high[rows, :], turned_low[rows, :], c)
+            pltpu.make_async_copy(first_left.at[pl.ds(0, 2)], first_left.at[pl.ds(0, 2)], first_left_sem).wait()
+            pltpu.make_async_copy(first_left.at[0], first_left.at[0], tail_sem).wait()
             for block in range(2):
-                pltpu.make_async_copy(first_left.at[block], first_left.at[block], first_left_sem.at[block]).wait()
-                right = jnp.concatenate([first_left[block, :, l, :] for l in range(8)], axis=0)
+                right = jnp.concatenate(
+                    [first_left[2 * block + k, :, l, :] for l in range(8) for k in range(2)], axis=0
+                )
                 right_high, right_low = halves(right)
                 high, low = halves(mixed_out[...].reshape(512, 512))
                 both = dot(jnp.concatenate([high, low], axis=0), right_high)
@@ -325,8 +351,12 @@
                     first = first_out[block, pl.ds(2 * d_pair, 64, stride=8), :]
                     second = first_out[block, pl.ds(2 * d_pair + 1, 64, stride=8), :]
                     lanes = slice(d_pair * 128, d_pair * 128 + 128)
-                    partial[0, block * 128:block * 128 + 64, lanes] = pair_even(first, second)
-                    partial[0, block * 128 + 64:block * 128 + 128, lanes] = pair_odd(first, second)
+                    even = pair_even(first, second)
+                    odd = pair_odd(first, second)
+                    for piece in range(8):
+                        start = piece * 32 + block * 16
+                        partial[0, start:start + 8, lanes] = even[piece * 8:piece * 8 + 8]
+                        partial[0, start + 8:start + 16, lanes] = odd[piece * 8:piece * 8 + 8]
 
         def place_rows(lattice_row, c):
             source = lattice_row - 1
@@ -349,23 +379,32 @@
                 mix(high, low, c)
                 if c > 0:
                     close(lattice_row, c - 1)
-            close(lattice_row, 3)
+            close(lattice_row, 3, 0, 64)
+            send_partial(lattice_row, 0, 2)
+            close(lattice_row, 3, 64, 192)
+            send_partial(lattice_row, 2, 8)
 
         def partial_copy(lattice_row, c, step):
             is_first = lattice_row == 0
             target = lax.rem(jnp.where(is_first, col, row) + step, 4)
-            rows = pl.ds(pl.multiple_of(target * 64 + c * 16, 16), 16)
+            rows = pl.ds(pl.multiple_of(c * 32 + target * 8, 8), 8)
             device = jnp.where(is_first, in_row(step), in_col(step))
             return remote(
                 partial.at[lattice_row, rows], partial_in.at[lattice_row, c, step - 1],
                 partial_send.at[lattice_row], partial_sem.at[lattice_row, c], (1, site, device),
             )
 
+        def send_partial(lattice_row, begin, end):
+            @pl.loop(begin, end)
+            def _(c):
+                for step in (2, 1, 3):
+                    partial_copy(lattice_row, c, step).start()
+
         def reduced(lattice_row, c):
             every = partial_in.at[lattice_row, c]
             pltpu.make_async_copy(every, every, partial_sem.at[lattice_row, c]).wait()
             own = jnp.where(lattice_row == 0, col, row)
-            rows = pl.ds(pl.multiple_of(own * 64 + c * 16, 16), 16)
+            rows = pl.ds(pl.multiple_of(c * 32 + own * 8, 8), 8)
             total = partial[lattice_row, rows, :]
             for k in range(3):
                 total = total + partial_in[lattice_row, c, k]
@@ -382,15 +421,11 @@
             @pl.when(lattice_row == 0)
             def _():
                 first_row()
+                send_partial(0, 0, 8)
 
             @pl.when(lattice_row > 0)
             def _():
                 later_row(lattice_row)
-
-            @pl.loop(0, 4)
-            def _(c):
-                for step in (2, 1, 3):
-                    partial_copy(lattice_row, c, step).start()
 
             @pl.when(lattice_row == 0)
             def _():
@@ -409,20 +444,22 @@
             def _():
                 prepare_right(lattice_row + 1)
 
-                @pl.loop(0, 4)
+                @pl.loop(0, 8)
                 def _(c):
-                    gathered[lattice_row, c, col] = reduced(lattice_row, c)
+                    rows = pl.ds(pl.multiple_of(lax.rem(c, 2) * 8, 8), 8)
+                    gathered[lattice_row, c // 2, col, rows, :] = reduced(lattice_row, c)
                     for step in (2, 1, 3):
                         gather_copy(lattice_row, c, step).start()
 
                 prepare_left(lattice_row + 1)
 
         slab_out().wait_send()
+        pltpu.make_async_copy(first_left.at[0], first_left.at[0], lead_send).wait()
         pltpu.make_async_copy(scale_in, scale_in, scale_sem).wait()
         inverse = scale_in[0:1, 0:1]
         acc = jnp.zeros((8, 128), F32)
         for c in range(4):
-            total = reduced(3, c) * inverse
+            total = jnp.concatenate([reduced(3, 2 * c), reduced(3, 2 * c + 1)], axis=0) * inverse
             acc = acc + fold(total)
 
             @pl.when(col == c)
@@ -432,12 +469,18 @@
             @pl.when(col != c)
             def _():
                 gathered[3, c, col] = total
-                final_copy(c).start()
+                if c < 3:
+                    final_copy(c).start()
 
         exchange_squares(acc)
+
+        @pl.when(col != 3)
+        def _():
+            final_copy(3).start()
+
         three = slab.at[pl.ds(0, 3)]
         pltpu.make_async_copy(three, three, slab_sem).wait()
-        write_out(inverse_scale())
+        write_out(inverse_scale)
 
         pltpu.make_async_copy(three, three, slab_send).wait()
         wait_squares_sent()
@@ -466,11 +509,11 @@
             pltpu.VMEM((8, 16, 256), F32),
             pltpu.VMEM((4, 16, 512), F32),
             pltpu.VMEM((16, 16, 512), F32),
-            pltpu.VMEM((2, 64, 8, 128), F32),
+            pltpu.VMEM((4, 32, 8, 128), F32),
             pltpu.VMEM((2, 512, 128), F32),
             pltpu.VMEM((2, 512, 128), F32),
             pltpu.VMEM((4, 4, 4, 16, 512), F32),
-            pltpu.VMEM((4, 4, 3, 16, 512), F32),
+            pltpu.VMEM((4, 8, 3, 8, 512), F32),
             pltpu.VMEM((4, 256, 512), F32),
             pltpu.VMEM((4, 16, 512), F32),
             pltpu.VMEM((16, 8, 128), F32),
@@ -490,8 +533,8 @@
             pltpu.VMEM((2, 128, 128), F32),
             pltpu.VMEM((4, 64, 1024), F32),
             pltpu.VMEM((4, 128, 512), F32),
-            dma, dma, dma((2,)), dma, pltpu.SemaphoreType.REGULAR,
-            dma((3, 4)), dma((4, 4)), dma, dma, dma,
+            dma, dma, dma, dma, dma((2,)), dma, dma, pltpu.SemaphoreType.REGULAR,
+            dma((3, 4)), dma((4, 8)), dma, dma, dma,
             dma((4, 4)), dma((4,)), dma((4,)), dma((2,)),
             pltpu.SemaphoreType.REGULAR,
             dma, dma((3,)), dma((4,)), dma, dma, dma,

time: 56.1 us -> 53.9 us (0.961)
  Pallas kernels: 55.4 us -> 53.2 us
    pallas_call x1, Pallas kernels: 55.4 us -> 53.2 us  [body(): pl.pallas_call(kernel, out_shape=jax.ShapeDtypeStruct((8, 16, 256), F32),...]
where the time goes in v3:
time: 53.9 us; the launch traced here: 53.8 us
  Pallas kernels  53.2 us (99%)
  local copies, waits for them, and re-layouts  0.66 us (1%)
    pallas_call x1, Pallas kernels, body(): pl.pallas_call(kernel, out_shape=jax.ShapeDtypeStruct((8, 16, 256), F32),...  53.2 us

profile of v3, /device:TPU:1, one launch (start us, length us, event | category | flops | bytes accessed | tf_op | source)
XLA Modules:
  0.0 53.8 jit_solution(5664899611103020243)
XLA Ops:
  0.0 53.2 %absorb.1 = f32[8,16,256]{2,1,0:T(8,128)S(1)} custom-call(f32[8,16,256]{2,1,0:T(8,128)} %bitcast.11, f32[2,256,8,256]{3,2,1,0:T(8,128)} %bitcast.9, f32[2,64,8,8]{3,2,1,0:T(8,128)} %bitcast.10), custom_call_target="tpu_custom_call" | custom-call | tf_op jit(solution)/shard_map/absorb/pallas_call | solution.py:503
  53.2 0.7 %copy.5 = f32[1,1,1,256,8,16]{3,5,4,2,1,0:T(8,128)} copy(f32[1,1,1,256,8,16]{3,5,4,2,1,0:T(8,128)S(1)} %bitcast.8) | data formatting | bytes 262144

commit v4 on v3

--- a/solution.py
+++ b/solution.py
@@ -160,15 +160,15 @@
     @pl.when(core == 0)
     def _():
         partner = (1, site, bond)
-        for k in range(3):
+        for k in (0, 2):
             quarter = lax.rem(row + k, 4)
-            lanes = pl.ds(pl.multiple_of((quarter // 2) * 128, 128), 128)
-            size = 16 if k == 0 else 32
+            lanes = pl.ds(pl.multiple_of(lax.rem(quarter, 2) * 128, 128), 128)
+            size = 8 if k == 0 else 32
             for start in range(0, 32, size):
-                rows = pl.ds(col * 64 + lax.rem(quarter, 2) * 32 + start, size)
+                rows = pl.ds(col * 64 + (quarter // 2) * 32 + start, size)
                 remote(
                     p_ref.at[0, rows, :, lanes], first_left.at[quarter, pl.ds(start, size)], first_left_send,
-                    lead_sem.at[start // 16] if k == 0 else first_left_sem, (1, next_site, bond),
+                    lead_sem.at[start // 8] if k == 0 else first_left_sem, (1, next_site, bond),
                 ).start()
         first_right = [
             remote(left_packed.at[0, pair], left_in.at[0, pair], left_send.at[0], left_sem.at[0, pair], partner)
@@ -206,7 +206,7 @@
         right_copy.wait_send()
         for k in range(2):
             mpo_copies[k].wait_send()
-        sent = first_left.at[pl.ds(0, 3)]
+        sent = first_left.at[pl.ds(0, 2)]
         pltpu.make_async_copy(sent, sent, first_left_send).wait()
 
     @pl.when(core == 1)
@@ -261,9 +261,11 @@
         for offset in far_first:
             first_copy(offset).start()
 
-        def mix(rows_high, rows_low, c):
+        def mix_left(rows_high, rows_low):
             both = dot(jnp.concatenate([rows_high, rows_low], axis=0), left_high[...])
-            left_part = both[0:128] + both[128:256] + dot(rows_high, left_low[...])
+            return both[0:128] + both[128:256] + dot(rows_high, left_low[...])
+
+        def mix_mpo(left_part, c):
             for pair in range(4):
                 lanes = slice(pair * 128, pair * 128 + 128)
                 first = left_part[0:64, lanes]
@@ -300,9 +302,31 @@
                 piece, piece, gather_send.at[lattice_row], gather_sem.at[lattice_row, c // 2], (1, site, in_row(step))
             )
 
-        def pass_on(k):
-            lead = first_left.at[row, pl.ds(k * 16, 16)]
-            return remote(lead, lead, lead_send, tail_sem, (1, site, in_col(1)))
+        def pass_on():
+            for k in range(4):
+                lead = first_left.at[row, pl.ds(k * 8, 8)]
+                pltpu.make_async_copy(lead, lead, lead_sem.at[k]).wait()
+                for step in (1, 3):
+                    remote(lead, lead, lead_send, tail_sem, (1, site, in_col(step))).start()
+
+        def close_first(k, block):
+            right = jnp.concatenate(
+                [first_left[block + half, :, l, :] for l in range(8) for half in (0, 2)], axis=0
+            )
+            right_high, right_low = halves(right)
+            high, low = halves(mixed_out[...].reshape(512, 512))
+            both = dot(jnp.concatenate([high, low], axis=0), right_high)
+            first_out[k] = both[0:512] + both[512:1024] + dot(high, right_low)
+            for d_pair in range(4):
+                first = first_out[k, pl.ds(2 * d_pair, 64, stride=8), :]
+                second = first_out[k, pl.ds(2 * d_pair + 1, 64, stride=8), :]
+                lanes = slice(d_pair * 128, d_pair * 128 + 128)
+                even = pair_even(first, second)
+                odd = pair_odd(first, second)
+                for piece in range(8):
+                    start = pl.multiple_of(piece * 32 + block * 16, 16)
+                    partial[0, pl.ds(start, 8), lanes] = even[piece * 8:piece * 8 + 8]
+                    partial[0, pl.ds(pl.multiple_of(start + 8, 8), 8), lanes] = odd[piece * 8:piece * 8 + 8]
 
         def first_row():
             for pair in range(4):
@@ -326,37 +350,23 @@
                 left_stage_copy(k).wait()
                 for pair in range(4):
                     pack_left(k, pair)
-            for k in range(2):
-                lead = first_left.at[row, pl.ds(k * 16, 16)]
-                pltpu.make_async_copy(lead, lead, lead_sem.at[k]).wait()
-                pass_on(k).start()
+            pass_on()
             pltpu.make_async_copy(first_in, first_in, first_sem).wait()
             high, low = halves(first_in[...].reshape(256, 512))
             left_high[...] = high
             left_low[...] = low
+            parts = []
             for c in range(4):
                 rows = slice(c * 128, c * 128 + 128)
-                mix(turned_high[rows, :], turned_low[rows, :], c)
-            pltpu.make_async_copy(first_left.at[pl.ds(0, 2)], first_left.at[pl.ds(0, 2)], first_left_sem).wait()
-            pltpu.make_async_copy(first_left.at[0], first_left.at[0], tail_sem).wait()
-            for block in range(2):
-                right = jnp.concatenate(
-                    [first_left[2 * block + k, :, l, :] for l in range(8) for k in range(2)], axis=0
-                )
-                right_high, right_low = halves(right)
-                high, low = halves(mixed_out[...].reshape(512, 512))
-                both = dot(jnp.concatenate([high, low], axis=0), right_high)
-                first_out[block] = both[0:512] + both[512:1024] + dot(high, right_low)
-                for d_pair in range(4):
-                    first = first_out[block, pl.ds(2 * d_pair, 64, stride=8), :]
-                    second = first_out[block, pl.ds(2 * d_pair + 1, 64, stride=8), :]
-                    lanes = slice(d_pair * 128, d_pair * 128 + 128)
-                    even = pair_even(first, second)
-                    odd = pair_odd(first, second)
-                    for piece in range(8):
-                        start = piece * 32 + block * 16
-                        partial[0, start:start + 8, lanes] = even[piece * 8:piece * 8 + 8]
-                        partial[0, start + 8:start + 16, lanes] = odd[piece * 8:piece * 8 + 8]
+                parts.append(mix_left(turned_high[rows, :], turned_low[rows, :]))
+                if c > 0:
+                    mix_mpo(parts[c - 1], c - 1)
+            mix_mpo(parts[3], 3)
+            near = lax.rem(row, 2)
+            pltpu.make_async_copy(first_left.at[0], first_left.at[0], first_left_sem).wait()
+            close_first(0, near)
+            pltpu.make_async_copy(first_left.at[pl.ds(0, 2)], first_left.at[pl.ds(0, 2)], tail_sem).wait()
+            close_first(1, 1 - near)
 
         def place_rows(lattice_row, c):
             source = lattice_row - 1
@@ -376,9 +386,10 @@
         def later_row(lattice_row):
             for c in range(4):
                 high, low = place_rows(lattice_row, c)
-                mix(high, low, c)
+                left_part = mix_left(high, low)
                 if c > 0:
                     close(lattice_row, c - 1)
+                mix_mpo(left_part, c)
             close(lattice_row, 3, 0, 64)
             send_partial(lattice_row, 0, 2)
             close(lattice_row, 3, 64, 192)
@@ -454,7 +465,7 @@
                 prepare_left(lattice_row + 1)
 
         slab_out().wait_send()
-        pltpu.make_async_copy(first_left.at[0], first_left.at[0], lead_send).wait()
+        pltpu.make_async_copy(first_left.at[pl.ds(0, 2)], first_left.at[pl.ds(0, 2)], lead_send).wait()
         pltpu.make_async_copy(scale_in, scale_in, scale_sem).wait()
         inverse = scale_in[0:1, 0:1]
         acc = jnp.zeros((8, 128), F32)
@@ -533,7 +544,7 @@
             pltpu.VMEM((2, 128, 128), F32),
             pltpu.VMEM((4, 64, 1024), F32),
             pltpu.VMEM((4, 128, 512), F32),
-            dma, dma, dma, dma, dma((2,)), dma, dma, pltpu.SemaphoreType.REGULAR,
+            dma, dma, dma, dma, dma((4,)), dma, dma, pltpu.SemaphoreType.REGULAR,
             dma((3, 4)), dma((4, 8)), dma, dma, dma,
             dma((4, 4)), dma((4,)), dma((4,)), dma((2,)),
             pltpu.SemaphoreType.REGULAR,

time: 53.9 us -> 53.3 us (0.989)
  Pallas kernels: 53.2 us -> 52.5 us
    pallas_call x1, Pallas kernels: 53.2 us -> 52.5 us  [body(): pl.pallas_call(kernel, out_shape=jax.ShapeDtypeStruct((8, 16, 256), F32),...]
where the time goes in v4:
time: 53.3 us; the launch traced here: 53.2 us
  Pallas kernels  52.5 us (98%)
  local copies, waits for them, and re-layouts  0.66 us (1%)
    pallas_call x1, Pallas kernels, body(): pl.pallas_call(kernel, out_shape=jax.ShapeDtypeStruct((8, 16, 256), F32),...  52.5 us

profile of v4, /device:TPU:1, one launch (start us, length us, event | category | flops | bytes accessed | tf_op | source)
XLA Modules:
  0.0 53.2 jit_solution(16671119898370487698)
XLA Ops:
  0.0 52.5 %absorb.1 = f32[8,16,256]{2,1,0:T(8,128)S(1)} custom-call(f32[8,16,256]{2,1,0:T(8,128)} %bitcast.11, f32[2,256,8,256]{3,2,1,0:T(8,128)} %bitcast.9, f32[2,64,8,8]{3,2,1,0:T(8,128)} %bitcast.10), custom_call_target="tpu_custom_call" | custom-call | tf_op jit(solution)/shard_map/absorb/pallas_call | solution.py:514
  52.5 0.7 %copy.5 = f32[1,1,1,256,8,16]{3,5,4,2,1,0:T(8,128)} copy(f32[1,1,1,256,8,16]{3,5,4,2,1,0:T(8,128)S(1)} %bitcast.8) | data formatting | bytes 262144

commit v5 on v4

--- a/solution.py
+++ b/solution.py
@@ -299,7 +299,7 @@
         def gather_copy(lattice_row, c, step):
             piece = gathered.at[lattice_row, c // 2, col, pl.ds(pl.multiple_of(lax.rem(c, 2) * 8, 8), 8)]
             return remote(
-                piece, piece, gather_send.at[lattice_row], gather_sem.at[lattice_row, c // 2], (1, site, in_row(step))
+                piece, piece, gather_send.at[lattice_row], gather_sem.at[lattice_row, c], (1, site, in_row(step))
             )
 
         def pass_on():
@@ -370,9 +370,9 @@
 
         def place_rows(lattice_row, c):
             source = lattice_row - 1
-            three = gathered.at[source, c, pl.ds(0, 3)]
-            pltpu.make_async_copy(three, three, gather_sem.at[source, c]).wait()
             for r0 in (0, 8):
+                three = gathered.at[source, c, pl.ds(0, 3), pl.ds(r0, 8)]
+                pltpu.make_async_copy(three, three, gather_sem.at[source, 2 * c + r0 // 8]).wait()
                 for pair in range(2):
                     for u_pair in range(4):
                         block = slice(u_pair * 128, u_pair * 128 + 128)
@@ -545,7 +545,7 @@
             pltpu.VMEM((4, 64, 1024), F32),
             pltpu.VMEM((4, 128, 512), F32),
             dma, dma, dma, dma, dma((4,)), dma, dma, pltpu.SemaphoreType.REGULAR,
-            dma((3, 4)), dma((4, 8)), dma, dma, dma,
+            dma((3, 8)), dma((4, 8)), dma, dma, dma,
             dma((4, 4)), dma((4,)), dma((4,)), dma((2,)),
             pltpu.SemaphoreType.REGULAR,
             dma, dma((3,)), dma((4,)), dma, dma, dma,

time: 53.3 us -> 53.7 us (level)
  no operation moved by 1% of the time
where the time goes in v5:
time: 53.7 us; the launch traced here: 53.6 us
  Pallas kernels  53 us (99%)
  local copies, waits for them, and re-layouts  0.66 us (1%)
    pallas_call x1, Pallas kernels, body(): pl.pallas_call(kernel, out_shape=jax.ShapeDtypeStruct((8, 16, 256), F32),...  53 us

profile of v5, /device:TPU:1, one launch (start us, length us, event | category | flops | bytes accessed | tf_op | source)
XLA Modules:
  0.0 53.6 jit_solution(2791684509017409776)
XLA Ops:
  0.0 53.0 %absorb.1 = f32[8,16,256]{2,1,0:T(8,128)S(1)} custom-call(f32[8,16,256]{2,1,0:T(8,128)} %bitcast.11, f32[2,256,8,256]{3,2,1,0:T(8,128)} %bitcast.9, f32[2,64,8,8]{3,2,1,0:T(8,128)} %bitcast.10), custom_call_target="tpu_custom_call" | custom-call | tf_op jit(solution)/shard_map/absorb/pallas_call | solution.py:514
  53.0 0.7 %copy.5 = f32[1,1,1,256,8,16]{3,5,4,2,1,0:T(8,128)} copy(f32[1,1,1,256,8,16]{3,5,4,2,1,0:T(8,128)S(1)} %bitcast.8) | data formatting | bytes 262144
